TPU v7x, 32 devices: a whole 2x2x4 slice. The times are simulated.
32 devices in a mesh: section: 4 (over z), row: 2 (over y), col: 4 (over x, core).
Axes of the slice: x: 2, y: 2, z: 4, core: 2. Of those that a mesh axis runs over, the one named last changes fastest.
Arguments:
- tokens: bfloat16 [4, 128, 3072], P('section', 'col', 'row'), may hold values from -6 to 6
- weights: bfloat16 [4, 3072, 12288], P('section', 'row', 'col'), may hold values from -0.109375 to 0.109375
- hidden_grads: bfloat16 [4, 128, 12288], P('section', 'row', 'col'), may hold values from -1.5 to 1.5
Outputs:
- hidden: bfloat16 [4, 128, 12288], P('section', 'row', 'col')
- weight_grad: bfloat16 [4, 3072, 12288], P('section', 'row', 'col')
- passed_grad: bfloat16 [4, 128, 3072], P('section', 'col', 'row')
All inputs are finite; a program needn't handle non-finite values.
Results may differ from a plain program's by a relative error of at most 0.0052.
Values may be sent and summed in bfloat16 or wider, within the bound.
No kernel may reach another device: no remote copies, remote signals or barrier semaphores. Data moves between devices by JAX's collectives and lax.ppermute only.
A program may use at most 64 MiB of HBM per device.

v0:
```python
import jax
import jax.numpy as jnp
from jax import lax
from jax.sharding import PartitionSpec as P


def shifted(value, axis, steps):
    count = lax.axis_size(axis)
    leading, last = (max(0, -steps), min(count, count - steps))
    return lax.ppermute(value, axis, [(source, source + steps) for source in range(leading, last)])


def on_device(tokens, weights, hidden_grads):
    token_tile = tokens[0]
    weight_tile = weights[0]
    grad_tile = hidden_grads[0]
    tokens_all = lax.all_gather(token_tile, "col", axis=0, tiled=True)
    hidden_sum = lax.psum_scatter(
        jnp.dot(tokens_all, weight_tile, preferred_element_type=jnp.float32).astype(jnp.bfloat16),
        "row",
        scatter_dimension=0,
        tiled=True,
    )
    grad_piece = lax.all_gather(grad_tile, "row", axis=0, tiled=True)
    weight_total = lax.dot_general(
        tokens_all, grad_piece, (((0,), (0,)), ((), ())), preferred_element_type=jnp.float32
    )
    input_piece = lax.dot_general(
        grad_piece, weight_tile, (((1,), (1,)), ((), ())), preferred_element_type=jnp.float32
    )
    weight_grad = weight_total.astype(jnp.bfloat16)
    input_grad = lax.psum_scatter(input_piece, "col", scatter_dimension=0, tiled=True).astype(
        jnp.bfloat16
    )
    passed_grad = shifted(input_grad, "section", -1)
    return (hidden_sum[None], weight_grad[None], passed_grad[None])


def solution(mesh):
    in_specs = (P("section", "col", "row"), P("section", "row", "col"), P("section", "row", "col"))
    out_specs = (P("section", "row", "col"), P("section", "row", "col"), P("section", "col", "row"))
    return jax.shard_map(
        on_device, mesh=mesh, in_specs=in_specs, out_specs=out_specs, check_vma=False
    )
```

profile of v0, /device:TPU:0, one launch (start us, length us, event | category | flops | bytes accessed | tf_op | source)
XLA Modules:
  0.0 80.7 jit_solution(3190279994158967588)
XLA Ops:
  7.2 0.0 copy-start
  7.2 0.0 reduce-scatter.5.cloned.1.call-start
  7.2 13.0 %all-gather.1 = bf16[1,128,3072]{2,1,0:T(8,128)(2,1)S(1)} all-gather(bf16[1,64,3072]{2,1,0:T(8,128)(2,1)} %param.5), channel_id=3, replica_groups=mesh['section'=4,'row'=2,'col'=4] {'row'}, dimensions={1}, use_global_device_ids=true | all-gather | bytes 1179648 | tf_op jit(solution)/shard_map/all_gather | solution.py:24
  20.2 7.8 %fusion.1 = f32[128,1536]{1,0:T(8,128)} fusion(bf16[1,1536,3072]{2,1,0:T(8,128)(2,1)} %param.4, bf16[1,128,3072]{2,1,0:T(8,128)(2,1)S(1)} %all-gather.1), kind=kOutput, calls=%fused_computation.2 | convolution fusion | flops 1207959552 | bytes 11010048 | tf_op jit(solution)/shard_map/dot_general | solution.py:28
  28.0 0.0 reduce-scatter.5.cloned.1.call-update
  28.0 0.0 reduce-scatter.3.cloned.1.call-start
  28.1 0.0 copy-done
  28.1 6.6 %all-gather = bf16[1,128,1536]{2,1,0:T(8,128)(2,1)S(1)} all-gather(bf16[1,32,1536]{2,1,0:T(8,128)(2,1)S(1)} %copy-done), channel_id=2, replica_groups=mesh['section'=4,'row'=2,'col'=4] {'col'}, dimensions={1}, use_global_device_ids=true | all-gather | bytes 491520 | tf_op jit(solution)/shard_map/all_gather | solution.py:17
  34.7 6.2 %fusion.5 = bf16[128,3072]{1,0:T(8,128)(2,1)} fusion(bf16[1,1536,3072]{2,1,0:T(8,128)(2,1)} %param.4, bf16[1,128,1536]{2,1,0:T(8,128)(2,1)S(1)} %all-gather), kind=kOutput, calls=%fused_computation.6 | convolution fusion | flops 1208352768 | bytes 10616832 | tf_op jit(solution)/shard_map/dot_general | solution.py:19
  41.0 0.0 reduce-scatter.3.cloned.1.call-update
  41.0 11.9 %reduce-scatter.5.cloned.1.call-done = f32[32,1536]{1,0:T(8,128)} async-done(((f32[128,1536]{1,0:T(8,128)}), f32[32,1536]{1,0:T(8,128)}) %reduce-scatter.5.cloned.1.call-update) | async-done | bytes 196624 | tf_op jit(solution)/shard_map/reduce_scatter | solution.py:32
  52.9 0.9 %convert_element_type.11 = bf16[32,1536]{1,0:T(8,128)(2,1)S(1)} convert(f32[32,1536]{1,0:T(8,128)} %reduce-scatter.5.cloned.1.call-done) | non-fusion elementwise | flops 49152 | bytes 294912 | tf_op jit(solution)/shard_map/convert_element_type | solution.py:32
  53.8 1.3 %collective-permute-start = (bf16[32,1536]{1,0:T(8,128)(2,1)S(1)}, bf16[32,1536]{1,0:T(8,128)(2,1)S(1)}, u32[]{:S(2)}, u32[]{:S(2)}) collective-permute-start(bf16[32,1536]{1,0:T(8,128)(2,1)S(1)} %convert_element_type.11), channel_id=1, source_target_pairs={{8,0},{16,8},{24,16},{9,1},{17,9},{25,17},{10,2},{18,10},{26,18},{... | collective-permute-start | bytes 294920 | tf_op jit(solution)/shard_map/ppermute | solution.py:10
  55.1 5.2 %fusion = bf16[1,1536,3072]{2,1,0:T(8,128)(2,1)} fusion(bf16[1,128,3072]{2,1,0:T(8,128)(2,1)S(1)} %all-gather.1, bf16[1,128,1536]{2,1,0:T(8,128)(2,1)S(1)} %all-gather), kind=kOutput, calls=%fused_computation.1 | convolution fusion | flops 1212678144 | bytes 10616832 | tf_op jit(solution)/shard_map/dot_general | solution.py:25
  60.3 0.0 collective-permute-done
  60.3 12.9 %reduce-scatter.3.cloned.1.call-done = bf16[64,3072]{1,0:T(8,128)(2,1)} async-done(((bf16[128,3072]{1,0:T(8,128)(2,1)}), bf16[64,3072]{1,0:T(8,128)(2,1)}) %reduce-scatter.3.cloned.1.call-update) | async-done | bytes 393232 | tf_op jit(solution)/shard_map/reduce_scatter | solution.py:18
  73.3 0.6 copy.7
Async XLA Ops:
  7.2 20.9 %copy-start = (bf16[1,32,1536]{2,1,0:T(8,128)(2,1)S(1)}, bf16[1,32,1536]{2,1,0:T(8,128)(2,1)}, u32[]{:S(2)}) copy-start(bf16[1,32,1536]{2,1,0:T(8,128)(2,1)} %param.3) | copy-start | bytes 294916
  7.2 45.7 %reduce-scatter.5.cloned.1.call-start = ((), (), s32[]{:S(2)}) async-start(), calls=%async_computation.3 | async-start | bytes 983040 | tf_op jit(solution)/shard_map/reduce_scatter | solution.py:32
  28.0 45.2 %reduce-scatter.3.cloned.1.call-start = ((), (), s32[]{:S(2)}) async-start(), calls=%async_computation.2 | async-start | bytes 1179648 | tf_op jit(solution)/shard_map/reduce_scatter | solution.py:18
  53.8 6.5 %collective-permute-start = (bf16[32,1536]{1,0:T(8,128)(2,1)S(1)}, bf16[32,1536]{1,0:T(8,128)(2,1)S(1)}, u32[]{:S(2)}, u32[]{:S(2)}) collective-permute-start(bf16[32,1536]{1,0:T(8,128)(2,1)S(1)} %convert_element_type.11), channel_id=1, source_target_pairs={{8,0},{16,8},{24,16},{9,1},{17,9},{25,17},{10,2},{18,10},{26,18},{... | collective-permute-start | bytes 294920 | tf_op jit(solution)/shard_map/ppermute | solution.py:10
Sparse Core Ops, SparseCore 0:
  28.2 24.6 reduce-scatter.4
  55.8 17.4 reduce-scatter.2
where the time goes:
time: 81 us; the launch traced here: 80.7 us
  waiting for transfers between devices  24.9 us (31%)
  blocking collectives  19.7 us (24%)
  matrix products  19.2 us (24%)
  between operations  14.1 us (17%)
  starting transfers between devices  1.37 us (2%)
  other arithmetic  0.94 us (1%)
    all_gather x1, blocking collectives, on_device(): grad_piece = lax.all_gather(grad_tile, 'row', axis=0, tiled=True)  13 us
    reduce_scatter x1, waiting for transfers between devices, on_device(): lax.psum_scatter(jnp.dot(tokens_all, weight_tile, preferred_element_type=...  12.9 us
    reduce_scatter x1, waiting for transfers between devices, on_device(): lax.psum_scatter(input_piece, 'col', scatter_dimension=0, tiled=True)  11.9 us
    dot_general x1, matrix products, on_device(): lax.dot_general(grad_piece, weight_tile, (((1,), (1,)), ((), ())), prefer...  7.78 us
    all_gather x1, blocking collectives, on_device(): tokens_all = lax.all_gather(token_tile, 'col', axis=0, tiled=True)  6.64 us
    dot_general x1, matrix products, on_device(): jnp.dot(tokens_all, weight_tile, preferred_element_type=jnp.float32)  6.23 us
    dot_general x1, matrix products, on_device(): lax.dot_general(tokens_all, grad_piece, (((0,), (0,)), ((), ())), preferr...  5.17 us
  transfers between devices with their start and end apart: 3, of which 2 were waited for; matrix products, arithmetic and copies ran while one was open for 15% of the time, Pallas kernels for 0%

commit v1 on v0

--- a/solution.py
+++ b/solution.py
@@ -2,6 +2,12 @@
 import jax.numpy as jnp
 from jax import lax
 from jax.sharding import PartitionSpec as P
+
+
+def press_rails(raw, dim_no):
+    m_next = list(raw.shape[1:])
+    m_next[dim_no] *= raw.shape[0]
+    return jnp.moveaxis(raw, 0, dim_no).reshape(m_next)
 
 
 def shifted(value, axis, steps):
@@ -14,7 +20,22 @@
     token_tile = tokens[0]
     weight_tile = weights[0]
     grad_tile = hidden_grads[0]
-    tokens_all = lax.all_gather(token_tile, "col", axis=0, tiled=True)
+    fan = lax.psum(1, "col")
+    slots = [(d, (d + 1) % fan) for d in range(fan)]
+    panels = [(t, c) for c, t in slots]
+    later, then = ([], [])
+    for w in tuple(range(fan - 1)):
+        if w % 2 == 0:
+            later.append(lax.ppermute(later[-1] if later else token_tile, "col", slots))
+        else:
+            block_last = lax.ppermute(then[-1] if then else token_tile, "col", panels)
+            then.append(block_last)
+    carry_in = jnp.stack([*later[::-1], token_tile, *then])
+    item_now = lax.axis_index("col")
+    kept_arr = len(later)
+    taken_in = item_now - kept_arr
+    carry_in = carry_in[(jnp.arange(fan) - taken_in) % fan]
+    tokens_all = press_rails(carry_in, 0)
     hidden_sum = lax.psum_scatter(
         jnp.dot(tokens_all, weight_tile, preferred_element_type=jnp.float32).astype(jnp.bfloat16),
         "row",

time: 81 us -> 81 us (level)
  blocking collectives: 19.7 us -> 13 us
  waiting for transfers between devices: 24.9 us -> 30.5 us
    ppermute x0 -> x3, waiting for transfers between devices: none -> 8.82 us  [the longest x2 8.82 us: on_device(): later.append(lax.ppermute(later[-1] if later else token_tile, 'col', slots))]
    all_gather x1 -> x0, blocking collectives: 6.64 us -> none  [on_device(): tokens_all = lax.all_gather(token_tile, 'col', axis=0, tiled=True)]
    reduce_scatter x1, waiting for transfers between devices: 11.9 us -> 8.71 us  [on_device(): lax.psum_scatter(input_piece, 'col', scatter_dimension=0, tiled=True)]
  transfers between devices with their start and end apart: 3 -> 6, of which waited for: 2 -> 4; matrix products, arithmetic and copies ran while one was open for 15% -> 16% of each run, Pallas kernels for 0% -> 0%
where the time goes in v1:
time: 81 us; the launch traced here: 80.7 us
  waiting for transfers between devices  30.5 us (38%)
  matrix products  18.9 us (23%)
  between operations  14.1 us (17%)
  blocking collectives  13 us (16%)
  starting transfers between devices  1.94 us (2%)
  local copies, waits for them, and re-layouts  1.22 us (2%)
  other arithmetic  1.01 us (1%)
    all_gather x1, blocking collectives, on_device(): grad_piece = lax.all_gather(grad_tile, 'row', axis=0, tiled=True)  13 us
    reduce_scatter x1, waiting for transfers between devices, on_device(): lax.psum_scatter(jnp.dot(tokens_all, weight_tile, preferred_element_type=...  12.9 us
    ppermute x2, waiting for transfers between devices, on_device(): later.append(lax.ppermute(later[-1] if later else token_tile, 'col', slots))  8.82 us
    reduce_scatter x1, waiting for transfers between devices, on_device(): lax.psum_scatter(input_piece, 'col', scatter_dimension=0, tiled=True)  8.71 us
    dot_general x1, matrix products, on_device(): lax.dot_general(grad_piece, weight_tile, (((1,), (1,)), ((), ())), prefer...  7.78 us
    dot_general x1, matrix products, on_device(): jnp.dot(tokens_all, weight_tile, preferred_element_type=jnp.float32)  5.98 us
    dot_general x1, matrix products, on_device(): lax.dot_general(tokens_all, grad_piece, (((0,), (0,)), ((), ())), preferr...  5.17 us
  transfers between devices with their start and end apart: 6, of which 4 were waited for; matrix products, arithmetic and copies ran while one was open for 16% of the time, Pallas kernels for 0%

profile of v1, /device:TPU:0, one launch (start us, length us, event | category | flops | bytes accessed | tf_op | source)
XLA Modules:
  0.0 80.7 jit_solution(4896896406643508303)
XLA Ops:
  7.2 0.0 copy-start
  7.2 0.0 reduce-scatter.5.cloned.1.call-start
  7.2 13.0 %all-gather = bf16[1,128,3072]{2,1,0:T(8,128)(2,1)S(1)} all-gather(bf16[1,64,3072]{2,1,0:T(8,128)(2,1)} %param.5), channel_id=2, replica_groups=mesh['section'=4,'row'=2,'col'=4] {'row'}, dimensions={1}, use_global_device_ids=true | all-gather | bytes 1179648 | tf_op jit(solution)/shard_map/all_gather | solution.py:45
  20.2 7.8 %fusion.1 = f32[128,1536]{1,0:T(8,128)} fusion(bf16[1,1536,3072]{2,1,0:T(8,128)(2,1)} %param.4, bf16[1,128,3072]{2,1,0:T(8,128)(2,1)S(1)} %all-gather), kind=kOutput, calls=%fused_computation.3 | convolution fusion | flops 1207959552 | bytes 11010048 | tf_op jit(solution)/shard_map/dot_general | solution.py:49
  28.0 0.0 reduce-scatter.5.cloned.1.call-update
  28.0 0.0 reduce-scatter.3.cloned.1.call-start
  28.1 0.0 copy-done
  28.1 0.3 collective-permute-start.2
  28.4 0.3 collective-permute-start
  28.7 4.8 %collective-permute-done = bf16[32,1536]{1,0:T(8,128)(2,1)S(1)} collective-permute-done((bf16[32,1536]{1,0:T(8,128)(2,1)S(1)}, bf16[32,1536]{1,0:T(8,128)(2,1)S(1)}, u32[]{:S(2)}, u32[]{:S(2)}) %collective-permute-start) | collective-permute-done | bytes 98336 | tf_op jit(solution)/shard_map/ppermute | solution.py:29
  33.5 0.0 collective-permute-start.1
  33.5 0.0 collective-permute-done.2
  33.5 4.0 %collective-permute-done.1 = bf16[32,1536]{1,0:T(8,128)(2,1)S(1)} collective-permute-done((bf16[32,1536]{1,0:T(8,128)(2,1)S(1)}, bf16[32,1536]{1,0:T(8,128)(2,1)S(1)}, u32[]{:S(2)}, u32[]{:S(2)}) %collective-permute-start.1) | collective-permute-done | bytes 98336 | tf_op jit(solution)/shard_map/ppermute | solution.py:29
  37.5 0.1 pad_maximum_fusion
  37.6 0.6 gather_fusion
  38.1 6.0 %fusion.5 = bf16[128,3072]{1,0:T(8,128)(2,1)} fusion(bf16[128,1536]{1,0:T(8,128)(2,1)S(1)} %bitcast.25, bf16[1,1536,3072]{2,1,0:T(8,128)(2,1)} %param.4), kind=kOutput, calls=%fused_computation.7 | convolution fusion | flops 1208352768 | bytes 10616832 | tf_op jit(solution)/shard_map/dot_general | solution.py:40
  44.1 0.0 reduce-scatter.3.cloned.1.call-update
  44.2 8.7 %reduce-scatter.5.cloned.1.call-done = f32[32,1536]{1,0:T(8,128)} async-done(((f32[128,1536]{1,0:T(8,128)}), f32[32,1536]{1,0:T(8,128)}) %reduce-scatter.5.cloned.1.call-update) | async-done | bytes 196624 | tf_op jit(solution)/shard_map/reduce_scatter | solution.py:53
  52.9 0.9 %convert_element_type.11 = bf16[32,1536]{1,0:T(8,128)(2,1)S(1)} convert(f32[32,1536]{1,0:T(8,128)} %reduce-scatter.5.cloned.1.call-done) | non-fusion elementwise | flops 49152 | bytes 294912 | tf_op jit(solution)/shard_map/convert_element_type | solution.py:53
  53.8 1.3 %collective-permute-start.3 = (bf16[32,1536]{1,0:T(8,128)(2,1)S(1)}, bf16[32,1536]{1,0:T(8,128)(2,1)S(1)}, u32[]{:S(2)}, u32[]{:S(2)}) collective-permute-start(bf16[32,1536]{1,0:T(8,128)(2,1)S(1)} %convert_element_type.11), channel_id=1, source_target_pairs={{8,0},{16,8},{24,16},{9,1},{17,9},{25,17},{10,2},{18,10},{26,18},{... | collective-permute-start | bytes 294920 | tf_op jit(solution)/shard_map/ppermute | solution.py:16
  55.1 5.2 %fusion = bf16[1,1536,3072]{2,1,0:T(8,128)(2,1)} fusion(bf16[128,1536]{1,0:T(8,128)(2,1)S(1)} %bitcast.26, bf16[1,128,3072]{2,1,0:T(8,128)(2,1)S(1)} %all-gather), kind=kOutput, calls=%fused_computation.2 | convolution fusion | flops 1212678144 | bytes 10616832 | tf_op jit(solution)/shard_map/dot_general | solution.py:46
  60.3 0.0 collective-permute-done.3
  60.3 12.9 %reduce-scatter.3.cloned.1.call-done = bf16[64,3072]{1,0:T(8,128)(2,1)} async-done(((bf16[128,3072]{1,0:T(8,128)(2,1)}), bf16[64,3072]{1,0:T(8,128)(2,1)}) %reduce-scatter.3.cloned.1.call-update) | async-done | bytes 393232 | tf_op jit(solution)/shard_map/reduce_scatter | solution.py:39
  73.3 0.6 copy.7
  (2 shorter events, 0.0 us)
Async XLA Ops:
  7.2 20.9 %copy-start = (bf16[1,32,1536]{2,1,0:T(8,128)(2,1)S(1)}, bf16[1,32,1536]{2,1,0:T(8,128)(2,1)}, u32[]{:S(2)}) copy-start(bf16[1,32,1536]{2,1,0:T(8,128)(2,1)} %param.3) | copy-start | bytes 294916
  7.2 45.7 %reduce-scatter.5.cloned.1.call-start = ((), (), s32[]{:S(2)}) async-start(), calls=%async_computation.3 | async-start | bytes 983040 | tf_op jit(solution)/shard_map/reduce_scatter | solution.py:53
  28.0 45.2 %reduce-scatter.3.cloned.1.call-start = ((), (), s32[]{:S(2)}) async-start(), calls=%async_computation.2 | async-start | bytes 1179648 | tf_op jit(solution)/shard_map/reduce_scatter | solution.py:39
  28.1 5.4 %collective-permute-start.2 = (bf16[32,1536]{1,0:T(8,128)(2,1)S(1)}, bf16[32,1536]{1,0:T(8,128)(2,1)S(1)}, u32[]{:S(2)}, u32[]{:S(2)}) collective-permute-start(bf16[32,1536]{1,0:T(8,128)(2,1)S(1)} %bitcast.27), channel_id=1, source_target_pairs={{1,0},{2,1},{3,2},{0,3},{5,4},{6,5},{7,6},{4,7},{9,8},{10,9},{11,1... | collective-permute-start | bytes 294920 | tf_op jit(solution)/shard_map/ppermute | solution.py:31
  28.4 5.1 %collective-permute-start = (bf16[32,1536]{1,0:T(8,128)(2,1)S(1)}, bf16[32,1536]{1,0:T(8,128)(2,1)S(1)}, u32[]{:S(2)}, u32[]{:S(2)}) collective-permute-start(bf16[32,1536]{1,0:T(8,128)(2,1)S(1)} %bitcast.28), channel_id=1, source_target_pairs={{0,1},{1,2},{2,3},{3,0},{4,5},{5,6},{6,7},{7,4},{8,9},{9,10},{10,1... | collective-permute-start | bytes 294920 | tf_op jit(solution)/shard_map/ppermute | solution.py:29
  33.5 4.0 %collective-permute-start.1 = (bf16[32,1536]{1,0:T(8,128)(2,1)S(1)}, bf16[32,1536]{1,0:T(8,128)(2,1)S(1)}, u32[]{:S(2)}, u32[]{:S(2)}) collective-permute-start(bf16[32,1536]{1,0:T(8,128)(2,1)S(1)} %collective-permute-done), channel_id=1, source_target_pairs={{0,1},{1,2},{2,3},{3,0},{4,5},{5,6},{6,7},{7,4},{8,9},{9,10},{10,1... | collective-permute-start | bytes 294920 | tf_op jit(solution)/shard_map/ppermute | solution.py:29
  53.8 6.5 %collective-permute-start.3 = (bf16[32,1536]{1,0:T(8,128)(2,1)S(1)}, bf16[32,1536]{1,0:T(8,128)(2,1)S(1)}, u32[]{:S(2)}, u32[]{:S(2)}) collective-permute-start(bf16[32,1536]{1,0:T(8,128)(2,1)S(1)} %convert_element_type.11), channel_id=1, source_target_pairs={{8,0},{16,8},{24,16},{9,1},{17,9},{25,17},{10,2},{18,10},{26,18},{... | collective-permute-start | bytes 294920 | tf_op jit(solution)/shard_map/ppermute | solution.py:16
Sparse Core Ops, SparseCore 0:
  28.2 24.6 reduce-scatter.4
  55.8 17.4 reduce-scatter.2
